TPU v7x, 128 devices: a whole 4x4x4 slice. The times are simulated.
128 devices in a mesh: row: 16 (over z, x_hi, core), col: 8 (over x_lo, y).
Axes of the slice: x: 4 (x_hi: 2, x_lo: 2; x = x_hi * 2 + x_lo), y: 4, z: 4, core: 2. Of those that a mesh axis runs over, the one named last changes fastest.
Arguments:
- stored: bfloat16 [1024, 51200], P(('row', 'col')), may hold values from -24 to 24
- integrals: bfloat16 [51200, 25600], P('row', 'col'), may hold values from -0.02734375 to 0.02734375
- layout: int32 [1024], replicated, may hold values from 0 to 1023, each once
- partner: int32 [1024], replicated, may hold values from 0 to 1023, as said below
Outputs:
- residual_out: bfloat16 [1024, 25600], P('row', 'col')
Inputs may be any that keep to these rules, and one draw needn't show every extreme that they name: partner is an involution without fixed points: partner[p] != p and partner[partner[p]] = p. `layout`: each slab pair stands in exactly one stored row.
All inputs are finite; a program needn't handle non-finite values.
Results may differ from a plain program's by a relative error of at most 0.001.
Values may be sent and summed in bfloat16 or wider, within the bound.
A program may use at most 128 MiB of HBM per device.

v0:
```python
import jax
import jax.numpy as jnp
from jax import lax
from jax.sharding import PartitionSpec as P


def per_device(stored, integrals, layout, partner):
    local_rows = stored.shape[0]
    n_row = lax.axis_size("row")
    n_col = lax.axis_size("col")
    total = local_rows * n_row * n_col
    regrouped = lax.all_to_all(stored, "row", split_axis=1, concat_axis=0, tiled=True)
    partial_sums = jnp.dot(
        lax.all_gather(regrouped, "col", axis=0, tiled=True),
        integrals,
        preferred_element_type=jnp.float32,
    )
    place = jnp.arange(total, dtype=jnp.int32)
    group_size = n_row * local_rows
    source_col = place // group_size
    remain = place % group_size
    source_row = remain // local_rows
    offset = remain % local_rows
    stored_index = (source_row * n_col + source_col) * local_rows + offset
    where_global = jnp.zeros((total,), jnp.int32).at[layout[stored_index]].set(place)
    difference = partial_sums[where_global] - partial_sums[where_global[partner]]
    return lax.psum_scatter(difference, "row", scatter_dimension=0, tiled=True).astype(jnp.bfloat16)


def solution(mesh):
    return jax.shard_map(
        per_device,
        mesh=mesh,
        in_specs=(P(("row", "col"), None), P("row", "col"), P(), P()),
        out_specs=P("row", "col"),
        check_vma=False,
    )
```

profile of v0, /device:TPU:1, one launch (start us, length us, event | category | flops | bytes accessed | tf_op | source)
XLA Modules:
  0.0 313.7 jit_solution(5771795690259070240)
XLA Ops:
  6.5 0.0 copy-start
  6.5 0.0 all-gather.2.cloned.1.call-start
  6.5 24.0 %all_to_all.19 = bf16[8,16,3200]{2,0,1:T(8,128)(2,1)} all-to-all(bf16[8,16,3200]{2,0,1:T(8,128)(2,1)} %bitcast.13), channel_id=1, replica_groups=mesh['row'=16,'col'=8] {'row'}, dimensions={1} | all-to-all | bytes 1638400 | tf_op jit(solution)/shard_map/all_to_all | solution.py:12
  30.6 0.0 all-gather.2.cloned.1.call-update
  30.6 0.0 reduce-scatter.2.cloned.1.call-start
  30.7 0.0 copy-done
  30.7 4.5 %gather_fusion = s32[1024]{0:T(1024)S(1)} fusion(s32[1024]{0:T(1024)S(1)} %copy-done, s32[1024]{0:T(1024)S(1)} %broadcast_clamp_fusion.1), kind=kCustom, calls=%fused_computation | custom fusion | bytes 12288 | tf_op jit(solution)/shard_map/gather | solution.py:25
  35.3 4.3 %scatter_custom_fusion = s32[1024]{0:T(1024)S(1)} fusion(s32[1024]{0:T(1024)S(1)} %bitcast.18, s32[1024]{0:T(1024)S(1)} %iota.7, s32[]{:T(128)} %constant.45.clone.1), kind=kCustom, calls=%fused_computation.27 | custom fusion | bytes 4100 | tf_op jit(solution)/shard_map/scatter | solution.py:25
  39.6 0.7 fusion.4
  40.3 4.5 %gather_fusion.2 = s32[1024]{0:T(1024)S(1)} fusion(s32[1024]{0:T(1024)S(1)} %scatter_custom_fusion, s32[1024]{0:T(1024)S(1)} %fusion.4), kind=kCustom, calls=%fused_computation.2 | custom fusion | bytes 12288 | tf_op jit(solution)/shard_map/gather | solution.py:26
  44.8 57.9 %all-gather.2.cloned.1.call-done = bf16[1024,3200]{1,0:T(8,128)(2,1)} async-done(((bf16[128,3200]{1,0:T(8,128)(2,1)}), bf16[1024,3200]{1,0:T(8,128)(2,1)}) %all-gather.2.cloned.1.call-update) | async-done | bytes 6553616 | tf_op jit(solution)/shard_map/all_gather | solution.py:14
  102.7 30.6 %fusion.7 = f32[1024,3200]{1,0:T(8,128)} fusion(bf16[1024,3200]{1,0:T(8,128)(2,1)} %all-gather.2.cloned.1.call-done, bf16[3200,3200]{1,0:T(8,128)(2,1)} %param.5), kind=kOutput, calls=%fused_computation.29 | convolution fusion | flops 20971520000 | bytes 40140800 | tf_op jit(solution)/shard_map/dot_general | solution.py:13
  133.3 17.1 %gather_fusion.3 = f32[1024,3200]{1,0:T(8,128)} fusion(f32[1024,3200]{1,0:T(8,128)} %fusion.7, s32[1024]{0:T(1024)S(1)} %broadcast_clamp_fusion), kind=kCustom, calls=%fused_computation.3 | custom fusion | bytes 26218496 | tf_op jit(solution)/shard_map/gather | solution.py:26
  150.4 17.1 %gather_fusion.1 = f32[1024,3200]{1,0:T(8,128)} fusion(f32[1024,3200]{1,0:T(8,128)} %fusion.7, s32[1024]{0:T(1024)S(1)} %fusion.3), kind=kCustom, calls=%fused_computation.1 | custom fusion | bytes 26218496 | tf_op jit(solution)/shard_map/gather | solution.py:26
  167.5 0.0 copy-start.1
  167.5 14.4 %sub.15 = f32[1024,3200]{1,0:T(8,128)} subtract(f32[1024,3200]{1,0:T(8,128)} %gather_fusion.1, f32[1024,3200]{1,0:T(8,128)} %gather_fusion.3) | non-fusion elementwise | flops 3276800 | bytes 39321600 | tf_op jit(solution)/shard_map/sub | solution.py:26
  181.8 0.0 reduce-scatter.2.cloned.1.call-update
  181.8 123.1 %reduce-scatter.2.cloned.1.call-done = f32[64,3200]{1,0:T(8,128)} async-done(((f32[1024,3200]{1,0:T(8,128)}), f32[64,3200]{1,0:T(8,128)}) %reduce-scatter.2.cloned.1.call-update) | async-done | bytes 819216 | tf_op jit(solution)/shard_map/reduce_scatter | solution.py:27
  305.0 1.9 convert_element_type.3
  306.9 0.0 copy-done.1
  (7 shorter events, 0.1 us)
Async XLA Ops:
  6.5 24.2 %copy-start = (s32[1024]{0:T(1024)S(1)}, s32[1024]{0:T(1024)}, u32[]{:S(2)}) copy-start(s32[1024]{0:T(1024)} %param.6) | copy-start | bytes 12292
  6.5 96.2 %all-gather.2.cloned.1.call-start = ((), (), s32[]{:S(2)}) async-start(), calls=%async_computation.2 | async-start | bytes 7372800 | tf_op jit(solution)/shard_map/all_gather | solution.py:14
  30.6 274.4 %reduce-scatter.2.cloned.1.call-start = ((), (), s32[]{:S(2)}) async-start(), calls=%async_computation.3 | async-start | bytes 13926400 | tf_op jit(solution)/shard_map/reduce_scatter | solution.py:27
  167.5 139.4 %copy-start.1 = (s32[1024]{0:T(1024)S(1)}, s32[1024]{0:T(1024)}, u32[]{:S(2)}) copy-start(s32[1024]{0:T(1024)} %param.6) | copy-start | bytes 12292
Sparse Core Ops, SparseCore 0:
  30.7 71.9 all-gather.1
  182.0 122.9 reduce-scatter.1
where the time goes:
time: 314 us
  waiting for transfers between devices  181 us (58%)
  local copies, waits for them, and re-layouts  47.5 us (15%)
  matrix products  30.6 us (10%)
  blocking collectives  24 us (8%)
  other arithmetic  17.1 us (5%)
  between operations  13.5 us (4%)
    reduce_scatter x1, waiting for transfers between devices, per_device(): lax.psum_scatter(difference, 'row', scatter_dimension=0, tiled=True)  123 us
    all_gather x1, waiting for transfers between devices, per_device(): lax.all_gather(regrouped, 'col', axis=0, tiled=True)  57.9 us
    dot_general x1, matrix products, per_device(): jnp.dot(lax.all_gather(regrouped, 'col', axis=0, tiled=True), integrals,...  30.6 us
    all_to_all x1, blocking collectives, per_device(): lax.all_to_all(stored, 'row', split_axis=1, concat_axis=0, tiled=True)  24 us
    gather x1, local copies, waits for them, and re-layouts, per_device(): partial_sums[where_global[partner]]  17.1 us
    gather x1, local copies, waits for them, and re-layouts, per_device(): partial_sums[where_global] - partial_sums[where_global[partner]]  17.1 us
    sub x1, other arithmetic, per_device(): partial_sums[where_global] - partial_sums[where_global[partner]]  14.4 us
  transfers between devices with their start and end apart: 2, of which 2 were waited for; matrix products, arithmetic and copies ran while one was open for 5% of the time, Pallas kernels for 0%

commit v1 on v0

--- a/solution.py
+++ b/solution.py
@@ -10,11 +10,19 @@
     n_col = lax.axis_size("col")
     total = local_rows * n_row * n_col
     regrouped = lax.all_to_all(stored, "row", split_axis=1, concat_axis=0, tiled=True)
-    partial_sums = jnp.dot(
-        lax.all_gather(regrouped, "col", axis=0, tiled=True),
-        integrals,
-        preferred_element_type=jnp.float32,
-    )
+
+    def node_scan(local):
+        return jnp.concatenate(
+            lax.all_to_all(
+                jnp.stack([local] * lax.axis_size("col")),
+                axis_name="col",
+                split_axis=0,
+                concat_axis=0,
+            ),
+            axis=0,
+        )
+
+    partial_sums = jnp.dot(node_scan(regrouped), integrals, preferred_element_type=jnp.float32)
     place = jnp.arange(total, dtype=jnp.int32)
     group_size = n_row * local_rows
     source_col = place // group_size

time: 314 us -> 322 us (1.025)
  starting transfers between devices: 0.04 us -> 4.82 us
  local copies, waits for them, and re-layouts: 47.5 us -> 51.1 us
    all_to_all x0 -> x1, waiting for transfers between devices: none -> 60.5 us  [node_scan(): lax.all_to_all(jnp.stack([local] * lax.axis_size('col')), axis_name='col'...]
    all_gather x1 -> x0, waiting for transfers between devices: 57.9 us -> none  [per_device(): lax.all_gather(regrouped, 'col', axis=0, tiled=True)]
    all_to_all x0 -> x1, starting transfers between devices: none -> 4.78 us  [node_scan(): lax.all_to_all(jnp.stack([local] * lax.axis_size('col')), axis_name='col'...]
    another operation x0 -> x1, local copies, waits for them, and re-layouts: none -> 3.53 us  [node_scan(): jnp.stack([local] * lax.axis_size('col'))]
  transfers between devices with their start and end apart: 2 -> 2, of which waited for: 2 -> 2; matrix products, arithmetic and copies ran while one was open for 5% -> 4% of each run, Pallas kernels for 0% -> 0%
where the time goes in v1:
time: 322 us
  waiting for transfers between devices  181 us (56%)
  local copies, waits for them, and re-layouts  51.1 us (16%)
  matrix products  30.6 us (10%)
  blocking collectives  23.9 us (7%)
  other arithmetic  16.4 us (5%)
  between operations  13.5 us (4%)
  starting transfers between devices  4.82 us (1%)
    reduce_scatter x1, waiting for transfers between devices, per_device(): lax.psum_scatter(difference, 'row', scatter_dimension=0, tiled=True)  121 us
    all_to_all x1, waiting for transfers between devices, node_scan(): lax.all_to_all(jnp.stack([local] * lax.axis_size('col')), axis_name='col'...  60.5 us
    dot_general x1, matrix products, per_device(): jnp.dot(node_scan(regrouped), integrals, preferred_element_type=jnp.float32)  30.6 us
    all_to_all x1, blocking collectives, per_device(): lax.all_to_all(stored, 'row', split_axis=1, concat_axis=0, tiled=True)  23.9 us
    gather x1, local copies, waits for them, and re-layouts, per_device(): partial_sums[where_global[partner]]  17.1 us
    gather x1, local copies, waits for them, and re-layouts, per_device(): partial_sums[where_global] - partial_sums[where_global[partner]]  17.1 us
    sub x1, other arithmetic, per_device(): partial_sums[where_global] - partial_sums[where_global[partner]]  14.4 us
  transfers between devices with their start and end apart: 2, of which 2 were waited for; matrix products, arithmetic and copies ran while one was open for 4% of the time, Pallas kernels for 0%

profile of v1, /device:TPU:1, one launch (start us, length us, event | category | flops | bytes accessed | tf_op | source)
XLA Modules:
  0.0 321.7 jit_solution(7081316567158587425)
XLA Ops:
  6.5 0.0 copy-start
  6.5 0.0 copy-start.2
  6.5 23.9 %all_to_all.21 = bf16[8,16,3200]{2,0,1:T(8,128)(2,1)S(1)} all-to-all(bf16[8,16,3200]{2,0,1:T(8,128)(2,1)} %bitcast.14), channel_id=1, replica_groups=mesh['row'=16,'col'=8] {'row'}, dimensions={1} | all-to-all | bytes 1638400 | tf_op jit(solution)/shard_map/all_to_all | solution.py:12
  30.5 3.5 %stack.5 = bf16[8,128,3200]{2,1,0:T(8,128)(2,1)} broadcast(bf16[128,3200]{1,0:T(8,128)(2,1)S(1)} %bitcast.13), dimensions={1,2} | broadcast | bytes 7372800 | tf_op jit(solution)/shard_map/stack | solution.py:17
  34.0 4.8 %all-to-all-start.1 = ((bf16[8,128,3200]{2,1,0:T(8,128)(2,1)}), bf16[8,128,3200]{2,1,0:T(8,128)(2,1)}, u32[]{:S(2)}, u32[]{:S(2)}) async-start(bf16[8,128,3200]{2,1,0:T(8,128)(2,1)} %stack.5), calls=%async_computation.1 | async-start | bytes 13107200 | tf_op jit(solution)/shard_map/all_to_all | solution.py:16
  38.8 0.0 reduce-scatter.2.cloned.1.call-start
  38.9 0.0 copy-done
  38.9 4.5 %gather_fusion = s32[1024]{0:T(1024)S(1)} fusion(s32[1024]{0:T(1024)S(1)} %copy-done, s32[1024]{0:T(1024)S(1)} %broadcast_clamp_fusion.1), kind=kCustom, calls=%fused_computation | custom fusion | bytes 12288 | tf_op jit(solution)/shard_map/gather | solution.py:33
  43.5 4.3 %scatter_custom_fusion = s32[1024]{0:T(1024)S(1)} fusion(s32[1024]{0:T(1024)S(1)} %bitcast.19, s32[1024]{0:T(1024)S(1)} %iota.7, s32[]{:T(128)} %constant.45.clone.1), kind=kCustom, calls=%fused_computation.27 | custom fusion | bytes 4100 | tf_op jit(solution)/shard_map/scatter | solution.py:33
  47.8 0.0 copy-done.2
  47.8 4.5 %gather_fusion.2 = s32[1024]{0:T(1024)S(1)} fusion(s32[1024]{0:T(1024)S(1)} %scatter_custom_fusion, s32[1024]{0:T(1024)S(1)} %fusion.4), kind=kCustom, calls=%fused_computation.2 | custom fusion | bytes 12288 | tf_op jit(solution)/shard_map/gather | solution.py:34
  52.4 60.5 %all-to-all-done.1 = bf16[8,128,3200]{2,1,0:T(8,128)(2,1)} async-done(((bf16[8,128,3200]{2,1,0:T(8,128)(2,1)}), bf16[8,128,3200]{2,1,0:T(8,128)(2,1)}, u32[]{:S(2)}, u32[]{:S(2)}) %all-to-all-start.1) | async-done | bytes 6553632 | tf_op jit(solution)/shard_map/all_to_all | solution.py:16
  112.9 30.6 %fusion.7 = f32[1024,3200]{1,0:T(8,128)} fusion(bf16[1024,3200]{1,0:T(8,128)(2,1)} %bitcast.3, bf16[3200,3200]{1,0:T(8,128)(2,1)} %param.5), kind=kOutput, calls=%fused_computation.29 | convolution fusion | flops 20971520000 | bytes 40140800 | tf_op jit(solution)/shard_map/dot_general | solution.py:25
  143.5 17.1 %gather_fusion.3 = f32[1024,3200]{1,0:T(8,128)} fusion(f32[1024,3200]{1,0:T(8,128)} %fusion.7, s32[1024]{0:T(1024)S(1)} %broadcast_clamp_fusion), kind=kCustom, calls=%fused_computation.3 | custom fusion | bytes 26218496 | tf_op jit(solution)/shard_map/gather | solution.py:34
  160.6 17.1 %gather_fusion.1 = f32[1024,3200]{1,0:T(8,128)} fusion(f32[1024,3200]{1,0:T(8,128)} %fusion.7, s32[1024]{0:T(1024)S(1)} %fusion.3), kind=kCustom, calls=%fused_computation.1 | custom fusion | bytes 26218496 | tf_op jit(solution)/shard_map/gather | solution.py:34
  177.6 0.0 copy-start.1
  177.7 14.4 %sub.15 = f32[1024,3200]{1,0:T(8,128)} subtract(f32[1024,3200]{1,0:T(8,128)} %gather_fusion.1, f32[1024,3200]{1,0:T(8,128)} %gather_fusion.3) | non-fusion elementwise | flops 3276800 | bytes 39321600 | tf_op jit(solution)/shard_map/sub | solution.py:34
  192.0 0.0 reduce-scatter.2.cloned.1.call-update
  192.0 120.9 %reduce-scatter.2.cloned.1.call-done = f32[64,3200]{1,0:T(8,128)} async-done(((f32[1024,3200]{1,0:T(8,128)}), f32[64,3200]{1,0:T(8,128)}) %reduce-scatter.2.cloned.1.call-update) | async-done | bytes 819216 | tf_op jit(solution)/shard_map/reduce_scatter | solution.py:35
  312.9 1.9 convert_element_type.3
  314.9 0.0 copy-done.1
  (8 shorter events, 0.1 us)
Async XLA Ops:
  6.5 32.4 %copy-start = (s32[1024]{0:T(1024)S(1)}, s32[1024]{0:T(1024)}, u32[]{:S(2)}) copy-start(s32[1024]{0:T(1024)} %param.6) | copy-start | bytes 12292
  6.5 41.2 %copy-start.2 = (s32[1024]{0:T(1024)S(1)}, s32[1024]{0:T(1024)}, u32[]{:S(2)}) copy-start(s32[1024]{0:T(1024)} %param.7) | copy-start | bytes 12292
  34.0 78.9 %all-to-all-start.1 = ((bf16[8,128,3200]{2,1,0:T(8,128)(2,1)}), bf16[8,128,3200]{2,1,0:T(8,128)(2,1)}, u32[]{:S(2)}, u32[]{:S(2)}) async-start(bf16[8,128,3200]{2,1,0:T(8,128)(2,1)} %stack.5), calls=%async_computation.1 | async-start | bytes 13107200 | tf_op jit(solution)/shard_map/all_to_all | solution.py:16
  38.8 274.1 %reduce-scatter.2.cloned.1.call-start = ((), (), s32[]{:S(2)}) async-start(), calls=%async_computation.3 | async-start | bytes 13926400 | tf_op jit(solution)/shard_map/reduce_scatter | solution.py:35
  177.6 137.2 %copy-start.1 = (s32[1024]{0:T(1024)S(1)}, s32[1024]{0:T(1024)}, u32[]{:S(2)}) copy-start(s32[1024]{0:T(1024)} %param.6) | copy-start | bytes 12292
Sparse Core Ops, SparseCore 0:
  192.2 120.7 reduce-scatter.1
